TPU v7x, 128 devices: a whole 4x4x4 slice. The times are simulated.
128 devices in a mesh: dp: 2 (over z_lo), head: 8 (over z_hi, y), tensor: 8 (over x, core).
Axes of the slice: x: 4, y: 4, z: 4 (z_hi: 2, z_lo: 2; z = z_hi * 2 + z_lo), core: 2. Of those that a mesh axis runs over, the one named last changes fastest.
Arguments:
- tokens: bfloat16 [512, 8192], P('dp', 'tensor'), may hold values from -6 to 6
- cotangent: bfloat16 [512, 8192], P('dp', 'tensor'), may hold values from -6 to 6
- w_gate: bfloat16 [8192, 29568], P('tensor', 'head'), may hold values from -0.0625 to 0.0625
- w_up: bfloat16 [8192, 29568], P('tensor', 'head'), may hold values from -0.0625 to 0.0625
- w_down: bfloat16 [29568, 8192], P('head', 'tensor'), may hold values from -0.03125 to 0.03125
- common_down_factor: bfloat16 [8192, 64], P('tensor'), may hold values from -0.0625 to 0.0625
- head_up: bfloat16 [64, 64, 8192], P('head', None, 'tensor'), may hold values from -0.0625 to 0.0625
- routes: int32 [512, 1], P('dp'), may hold values from 0 to 63
Outputs:
- grad_x: bfloat16 [512, 8192], P(('dp', 'head'), 'tensor')
- grad_shared: float32 [8192, 64], P('tensor')
- up_head_gradients: float32 [64, 64, 8192], P('head', None, 'tensor')
Inputs may be any that keep to these rules, and one draw needn't show every extreme that they name: `routes`: each token names one adapter head; the loads are skewed.
All inputs are finite; a program needn't handle non-finite values.
Results may differ from a plain program's by a relative error of at most 0.015.
Values may be sent and summed in bfloat16 or wider, within the bound.
A program may use at most 128 MiB of HBM per device.

v0:
```python
import jax
import jax.numpy as jnp
from jax import lax
from jax.sharding import PartitionSpec as P

ADAPTER_SCALE = 2.0


def contract_last(left, right):
    return lax.dot_general(
        left, right, (((1,), (1,)), ((), ())), preferred_element_type=jnp.float32
    )


def local(tokens, cotangent, w_gate, w_up, w_down, common_down_factor, head_up, routes):
    tok_rows, d_cols = tokens.shape
    hidden_activation = w_gate.shape[1]
    reduced_activation = common_down_factor.shape[1]
    local_heads = head_up.shape[0]
    first_head = lax.axis_index("head") * local_heads
    assigned_mask = (
        routes == first_head + jnp.arange(local_heads, dtype=jnp.int32)[None, :]
    ).astype(jnp.float32)
    flat_heads = head_up.reshape(local_heads * reduced_activation, d_cols)
    gate_preactivation = jnp.dot(tokens, w_gate, preferred_element_type=jnp.float32)
    up_preactivation = jnp.dot(tokens, w_up, preferred_element_type=jnp.float32)
    returned_gradient = contract_last(cotangent, w_down)
    adapter_selectors = jnp.dot(tokens, common_down_factor, preferred_element_type=jnp.float32)
    head_separated = contract_last(cotangent, flat_heads).reshape(
        tok_rows, local_heads, reduced_activation
    )
    selector_gradient = ADAPTER_SCALE * jnp.sum(head_separated * assigned_mask[:, :, None], axis=1)
    combined_total = lax.psum(
        jnp.concatenate(
            [
                gate_preactivation,
                up_preactivation,
                returned_gradient,
                adapter_selectors,
                selector_gradient,
            ],
            axis=1,
        ),
        "tensor",
    )
    gate_preactivation = combined_total[:, :hidden_activation]
    up_preactivation = combined_total[:, hidden_activation : 2 * hidden_activation]
    returned_gradient = combined_total[:, 2 * hidden_activation : 3 * hidden_activation]
    adapter_selectors = combined_total[
        :, 3 * hidden_activation : 3 * hidden_activation + reduced_activation
    ].astype(jnp.bfloat16)
    selector_gradient = combined_total[:, 3 * hidden_activation + reduced_activation :].astype(
        jnp.bfloat16
    )
    sig_gate = jax.nn.sigmoid(gate_preactivation)
    gate_gradient = (
        returned_gradient
        * up_preactivation
        * sig_gate
        * (1.0 + gate_preactivation * (1.0 - sig_gate))
    ).astype(jnp.bfloat16)
    up_gradient = (returned_gradient * gate_preactivation * sig_gate).astype(jnp.bfloat16)
    gate_gradient, up_gradient, adapter_selectors, selector_gradient = (
        gate_gradient,
        up_gradient,
        adapter_selectors,
        selector_gradient,
    )
    ffn_part = contract_last(gate_gradient, w_gate) + contract_last(up_gradient, w_up)
    own_ffn, own_code = (
        lax.psum_scatter(ffn_part, "head", scatter_dimension=0, tiled=True),
        lax.psum_scatter(
            selector_gradient.astype(jnp.float32), "head", scatter_dimension=0, tiled=True
        ),
    )
    grad_x = (own_ffn + contract_last(own_code.astype(jnp.bfloat16), common_down_factor)).astype(
        jnp.bfloat16
    )
    selector_mask = (
        adapter_selectors[:, None, :] * assigned_mask[:, :, None].astype(jnp.bfloat16)
    ).reshape(tok_rows, local_heads * reduced_activation)
    head_contributions = ADAPTER_SCALE * lax.dot_general(
        selector_mask, cotangent, (((0,), (0,)), ((), ())), preferred_element_type=jnp.float32
    )
    up_head_gradients = lax.psum(
        head_contributions.reshape(local_heads, reduced_activation, d_cols).astype(jnp.bfloat16),
        "dp",
    ).astype(jnp.float32)
    shared_term = lax.dot_general(
        tokens, selector_gradient, (((0,), (0,)), ((), ())), preferred_element_type=jnp.float32
    )
    grad_shared = lax.psum(shared_term.astype(jnp.bfloat16), ("dp", "head")).astype(jnp.float32)
    return (grad_x, grad_shared, up_head_gradients)


def solution(mesh):
    placed = (
        P("dp", "tensor"),
        P("dp", "tensor"),
        P("tensor", "head"),
        P("tensor", "head"),
        P("head", "tensor"),
        P("tensor", None),
        P("head", None, "tensor"),
        P("dp", None),
    )
    return jax.shard_map(
        local,
        mesh=mesh,
        in_specs=placed,
        out_specs=(P(("dp", "head"), "tensor"), P("tensor", None), P("head", None, "tensor")),
        check_vma=False,
    )
```

profile of v0, /device:TPU:0, one launch (start us, length us, event | category | flops | bytes accessed | tf_op | source)
XLA Modules:
  0.0 459.9 jit_solution(7197060639671306123)
XLA Ops:
  7.3 0.9 fusion.15
  8.2 7.9 %convolution_dynamic-update-slice_fusion.2 = f32[256,11216]{0,1:T(8,128)} fusion(bf16[256,1024]{1,0:T(8,128)(2,1)} %param.8, bf16[1024,3696]{0,1:T(8,128)(2,1)} %param.10), kind=kOutput, calls=%fused_computation.2 | convolution fusion | flops 1937768448 | bytes 11878400 | tf_op jit(solution)/shard_map/dot_general | solution.py:25
  16.1 4.3 convolution_dynamic-update-slice_fusion.1
  20.4 0.5 fusion.9
  20.9 4.3 convolution_dynamic-update-slice_fusion
  25.2 0.9 convolution_dynamic-update-slice_fusion.3
  26.1 0.6 multiply_dynamic-update-slice_fusion
  26.8 135.7 %all-reduce.4.cloned.1.call-done = f32[256,11216]{0,1:T(8,128)} async-done(((f32[256,11216]{0,1:T(8,128)}), f32[256,11216]{0,1:T(8,128)}) %all-reduce.4.cloned.1.call-update) | async-done | bytes 11485200 | tf_op jit(solution)/shard_map/psum | solution.py:33
  162.5 4.8 %convert.4 = bf16[256,11216]{0,1:T(8,128)(2,1)S(1)} convert(f32[256,11216]{0,1:T(8,128)} %all-reduce.4.cloned.1.call-done) | non-fusion elementwise | flops 2871296 | bytes 17227776 | tf_op jit(solution)/shard_map/convert.1
  167.4 2.4 copy-done.1
  169.8 0.9 fusion.10
  170.7 0.8 fusion.18
  171.5 0.8 copy.13
  172.4 1.4 multiply_convert_fusion.1
  174.1 7.7 %fusion.3 = f32[256,1024]{1,0:T(8,128)S(1)} fusion(bf16[1024,3696]{0,1:T(8,128)(2,1)} %param.11, f32[256,11216]{0,1:T(8,128)} %all-reduce.4.cloned.1.call-done), kind=kOutput, calls=%fused_computation.10 | convolution fusion | flops 1943445504 | bytes 16187392 | tf_op jit(solution)/shard_map/dot_general | solution.py:10
  181.7 10.2 %fusion.6 = f32[256,1024]{1,0:T(8,128)} fusion(f32[256,1024]{1,0:T(8,128)S(1)} %fusion.3, bf16[1024,3696]{0,1:T(8,128)(2,1)} %param.10, f32[256,11216]{0,1:T(8,128)} %all-reduce.4.cloned.1.call-done), kind=kOutput, calls=%fused_computation.12 | convolution fusion | flops 1947492352 | bytes 21020672 | tf_op jit(solution)/shard_map/dot_general | solution.py:10
  192.0 61.1 %all-reduce.6.cloned.1.call-done = bf16[1024,64]{0,1:T(8,128)(2,1)} async-done(((bf16[1024,64]{0,1:T(8,128)(2,1)}), bf16[1024,64]{0,1:T(8,128)(2,1)}) %all-reduce.6.cloned.1.call-update) | async-done | bytes 131088 | tf_op jit(solution)/shard_map/psum | solution.py:92
  253.1 1.6 convert_element_type.61
  254.7 71.5 %reduce-scatter.7.cloned.1.call-done = f32[32,64]{1,0:T(8,128)} async-done(((f32[256,64]{1,0:T(8,128)}), f32[32,64]{1,0:T(8,128)}) %reduce-scatter.7.cloned.1.call-update) | async-done | bytes 8208
  326.2 0.8 copy.14
  327.0 48.0 %all-reduce.8.cloned.1.call-done = bf16[8,64,1024]{2,1,0:T(8,128)(2,1)} async-done(((bf16[8,64,1024]{2,1,0:T(8,128)(2,1)}), bf16[8,64,1024]{2,1,0:T(8,128)(2,1)}) %all-reduce.8.cloned.1.call-update) | async-done | bytes 1048592 | tf_op jit(solution)/shard_map/psum | solution.py:85
  375.0 2.8 convert_element_type.65
  377.8 73.9 %reduce-scatter.5.cloned.1.call-done = f32[32,1024]{1,0:T(8,128)} async-done(((f32[256,1024]{1,0:T(8,128)}), f32[32,1024]{1,0:T(8,128)}) %reduce-scatter.5.cloned.1.call-update) | async-done | bytes 131088 | tf_op jit(solution)/shard_map/reduce_scatter | solution.py:71
  451.7 1.7 fusion.11
  (28 shorter events, 0.5 us)
Async XLA Ops:
  7.2 13.2 %copy-start = (bf16[8,64,1024]{2,1,0:T(8,128)(2,1)S(1)}, bf16[8,64,1024]{2,1,0:T(8,128)(2,1)}, u32[]{:S(2)}) copy-start(bf16[8,64,1024]{2,1,0:T(8,128)(2,1)} %param.14) | copy-start | bytes 3145732
  7.2 8.9 %copy-start.2 = (bf16[256,1024]{1,0:T(8,128)(2,1)S(1)}, bf16[256,1024]{1,0:T(8,128)(2,1)}, u32[]{:S(2)}) copy-start(bf16[256,1024]{1,0:T(8,128)(2,1)} %param.8) | copy-start | bytes 1572868
  7.2 155.3 %all-reduce.4.cloned.1.call-start = ((), (), s32[]{:S(2)}) async-start(), calls=%async_computation.2 | async-start | bytes 22970368 | tf_op jit(solution)/shard_map/psum | solution.py:33
  7.2 8.8 %copy-start.5 = (bf16[1024,3696]{0,1:T(8,128)(2,1)S(1)}, bf16[1024,3696]{0,1:T(8,128)(2,1)}, u32[]{:S(2)}) copy-start(bf16[1024,3696]{0,1:T(8,128)(2,1)} %param.11) | copy-start | bytes 22708228
  8.2 12.7 %slice-start = ((s8[7569408]{0:T(1024)(128)(4,1)}), s8[4194304]{0:T(1024)(128)(4,1)S(1)}, s32[]{:S(2)}) async-start(s8[7569408]{0:T(1024)(128)(4,1)} %bitcast.28), calls=%async_computation.7 | async-start | bytes 8388608
  16.1 4.3 copy-start.3
  16.1 4.8 %slice-start.1 = ((s8[7569408]{0:T(1024)(128)(4,1)}), s8[3375104]{0:T(1024)(128)(4,1)S(1)}, s32[]{:S(2)}) async-start(s8[7569408]{0:T(1024)(128)(4,1)} %bitcast.28), calls=%async_computation.8 | async-start | bytes 6750208
  20.4 4.8 %copy-start.4 = (bf16[1024,64]{0,1:T(8,128)(2,1)S(1)}, bf16[1024,64]{0,1:T(8,128)(2,1)}, u32[]{:S(2)}) copy-start(bf16[1024,64]{0,1:T(8,128)(2,1)} %param.13) | copy-start | bytes 393220
  26.8 226.4 %all-reduce.6.cloned.1.call-start = ((), (), s32[]{:S(2)}) async-start(), calls=%async_computation.4 | async-start | bytes 262144 | tf_op jit(solution)/shard_map/psum | solution.py:92
  167.4 2.5 copy-start.1
  170.7 155.5 %reduce-scatter.7.cloned.1.call-start = ((), (), s32[]{:S(2)}) async-start(), calls=%async_computation.6 | async-start | bytes 147456
  172.3 202.7 %all-reduce.8.cloned.1.call-start = ((), (), s32[]{:S(2)}) async-start(), calls=%async_computation.5 | async-start | bytes 2097152 | tf_op jit(solution)/shard_map/psum | solution.py:85
  173.8 277.9 %reduce-scatter.5.cloned.1.call-start = ((), (), s32[]{:S(2)}) async-start(), calls=%async_computation.3 | async-start | bytes 1179648 | tf_op jit(solution)/shard_map/reduce_scatter | solution.py:71
Sparse Core Ops, SparseCore 0:
  26.9 135.6 all-reduce.3
  170.8 82.2 all-reduce.5
  257.1 69.0 reduce-scatter.6
  329.2 45.7 all-reduce.7
  378.5 73.1 reduce-scatter.4
where the time goes:
time: 460 us
  waiting for transfers between devices  390 us (85%)
  matrix products  39.8 us (9%)
  between operations  13.9 us (3%)
  other arithmetic  11.6 us (3%)
    psum x1, waiting for transfers between devices, local(): lax.psum(jnp.concatenate([gate_preactivation, up_preactivation, returned_...  136 us
    reduce_scatter x1, waiting for transfers between devices, local(): lax.psum_scatter(ffn_part, 'head', scatter_dimension=0, tiled=True)  73.9 us
    unnamed x6, waiting for transfers between devices  71.5 us
    psum x1, waiting for transfers between devices, local(): lax.psum(shared_term.astype(jnp.bfloat16), ('dp', 'head'))  61.1 us
    psum x1, waiting for transfers between devices, local(): lax.psum(head_contributions.reshape(local_heads, reduced_activation, d_co...  48 us
    dot_general x5, matrix products, contract_last(): lax.dot_general(left, right, (((1,), (1,)), ((), ())), preferred_element_...  24.4 us
  transfers between devices with their start and end apart: 5, of which 5 were waited for; matrix products, arithmetic and copies ran while one was open for 6% of the time, Pallas kernels for 0%

commit v1 on v0

--- a/solution.py
+++ b/solution.py
@@ -4,6 +4,12 @@
 from jax.sharding import PartitionSpec as P
 
 ADAPTER_SCALE = 2.0
+
+
+def add_all(x, axis):
+    blocks = lax.all_gather(x, axis, axis=0, tiled=False)
+    total = blocks.sum(axis=0)
+    return total
 
 
 def contract_last(left, right):
@@ -82,7 +88,7 @@
     head_contributions = ADAPTER_SCALE * lax.dot_general(
         selector_mask, cotangent, (((0,), (0,)), ((), ())), preferred_element_type=jnp.float32
     )
-    up_head_gradients = lax.psum(
+    up_head_gradients = add_all(
         head_contributions.reshape(local_heads, reduced_activation, d_cols).astype(jnp.bfloat16),
         "dp",
     ).astype(jnp.float32)

time: 460 us -> 448 us (0.974)
  waiting for transfers between devices: 390 us -> 378 us
    psum x1 -> x0, waiting for transfers between devices: 48 us -> none  [local(): lax.psum(head_contributions.reshape(local_heads, reduced_activation, d_co...]
    all_gather x0 -> x1, waiting for transfers between devices: none -> 36.1 us  [add_all(): blocks = lax.all_gather(x, axis, axis=0, tiled=False)]
where the time goes in v1:
time: 448 us
  waiting for transfers between devices  378 us (84%)
  matrix products  39 us (9%)
  between operations  13.9 us (3%)
  other arithmetic  12.5 us (3%)
    psum x1, waiting for transfers between devices, local(): lax.psum(jnp.concatenate([gate_preactivation, up_preactivation, returned_...  136 us
    reduce_scatter x1, waiting for transfers between devices, local(): lax.psum_scatter(ffn_part, 'head', scatter_dimension=0, tiled=True)  73.3 us
    unnamed x6, waiting for transfers between devices  71.5 us
    psum x1, waiting for transfers between devices, local(): lax.psum(shared_term.astype(jnp.bfloat16), ('dp', 'head'))  61.2 us
    all_gather x1, waiting for transfers between devices, add_all(): blocks = lax.all_gather(x, axis, axis=0, tiled=False)  36.1 us
    dot_general x5, matrix products, contract_last(): lax.dot_general(left, right, (((1,), (1,)), ((), ())), preferred_element_...  24.2 us
  transfers between devices with their start and end apart: 5, of which 5 were waited for; matrix products, arithmetic and copies ran while one was open for 6% of the time, Pallas kernels for 0%

profile of v1, /device:TPU:0, one launch (start us, length us, event | category | flops | bytes accessed | tf_op | source)
XLA Modules:
  0.0 447.8 jit_solution(8860323344245272787)
XLA Ops:
  7.2 0.8 fusion.15
  8.1 7.5 %convolution_dynamic-update-slice_fusion.2 = f32[256,11216]{0,1:T(8,128)} fusion(bf16[256,1024]{1,0:T(8,128)(2,1)} %param.8, bf16[1024,3696]{0,1:T(8,128)(2,1)} %param.10), kind=kOutput, calls=%fused_computation.2 | convolution fusion | flops 1937768448 | bytes 11878400 | tf_op jit(solution)/shard_map/dot_general | solution.py:31
  15.6 4.1 convolution_dynamic-update-slice_fusion.1
  20.3 4.1 convolution_dynamic-update-slice_fusion
  24.4 0.9 convolution_dynamic-update-slice_fusion.3
  25.3 0.6 multiply_dynamic-update-slice_fusion
  26.0 135.7 %all-reduce.3.cloned.1.call-done = f32[256,11216]{0,1:T(8,128)} async-done(((f32[256,11216]{0,1:T(8,128)}), f32[256,11216]{0,1:T(8,128)}) %all-reduce.3.cloned.1.call-update) | async-done | bytes 11485200 | tf_op jit(solution)/shard_map/psum | solution.py:39
  161.8 4.8 %convert.5 = bf16[256,11216]{0,1:T(8,128)(2,1)S(1)} convert(f32[256,11216]{0,1:T(8,128)} %all-reduce.3.cloned.1.call-done) | non-fusion elementwise | flops 2871296 | bytes 17227776 | tf_op jit(solution)/shard_map/convert.2
  166.6 2.4 copy-done.1
  169.0 0.9 fusion.10
  170.0 0.8 fusion.18
  170.8 0.8 copy.13
  171.6 1.4 multiply_convert_fusion.1
  173.3 7.7 %fusion.3 = f32[256,1024]{1,0:T(8,128)S(1)} fusion(bf16[1024,3696]{0,1:T(8,128)(2,1)} %param.11, f32[256,11216]{0,1:T(8,128)} %all-reduce.3.cloned.1.call-done), kind=kOutput, calls=%fused_computation.10 | convolution fusion | flops 1943445504 | bytes 16187392 | tf_op jit(solution)/shard_map/dot_general | solution.py:16
  181.0 10.2 %fusion.6 = f32[256,1024]{1,0:T(8,128)} fusion(f32[256,1024]{1,0:T(8,128)S(1)} %fusion.3, bf16[1024,3696]{0,1:T(8,128)(2,1)} %param.10, f32[256,11216]{0,1:T(8,128)} %all-reduce.3.cloned.1.call-done), kind=kOutput, calls=%fused_computation.12 | convolution fusion | flops 1947492352 | bytes 21020672 | tf_op jit(solution)/shard_map/dot_general | solution.py:16
  191.2 61.2 %all-reduce.5.cloned.1.call-done = bf16[1024,64]{0,1:T(8,128)(2,1)} async-done(((bf16[1024,64]{0,1:T(8,128)(2,1)}), bf16[1024,64]{0,1:T(8,128)(2,1)}) %all-reduce.5.cloned.1.call-update) | async-done | bytes 131088 | tf_op jit(solution)/shard_map/psum | solution.py:98
  252.4 1.6 convert_element_type.70
  254.0 71.5 %reduce-scatter.7.cloned.1.call-done = f32[32,64]{1,0:T(8,128)} async-done(((f32[256,64]{1,0:T(8,128)}), f32[32,64]{1,0:T(8,128)}) %reduce-scatter.7.cloned.1.call-update) | async-done | bytes 8208
  325.4 0.8 copy.14
  326.3 36.1 %all-gather.2.cloned.1.call-done = bf16[2,8,64,1024]{3,2,1,0:T(8,128)(2,1)} async-done(((bf16[1,8,64,1024]{3,2,1,0:T(8,128)(2,1)}), bf16[2,8,64,1024]{3,2,1,0:T(8,128)(2,1)}) %all-gather.2.cloned.1.call-update) | async-done | bytes 2097168 | tf_op jit(solution)/shard_map/all_gather | solution.py:10
  362.4 2.2 reduce_sum.22
  364.6 1.6 convert_element_type.74
  366.2 73.3 %reduce-scatter.5.cloned.1.call-done = f32[32,1024]{1,0:T(8,128)} async-done(((f32[256,1024]{1,0:T(8,128)}), f32[32,1024]{1,0:T(8,128)}) %reduce-scatter.5.cloned.1.call-update) | async-done | bytes 131088 | tf_op jit(solution)/shard_map/reduce_scatter | solution.py:77
  439.5 1.7 fusion.11
  (29 shorter events, 1.0 us)
Async XLA Ops:
  7.2 12.6 %copy-start = (bf16[8,64,1024]{2,1,0:T(8,128)(2,1)S(1)}, bf16[8,64,1024]{2,1,0:T(8,128)(2,1)}, u32[]{:S(2)}) copy-start(bf16[8,64,1024]{2,1,0:T(8,128)(2,1)} %param.14) | copy-start | bytes 3145732
  7.2 154.6 %all-reduce.3.cloned.1.call-start = ((), (), s32[]{:S(2)}) async-start(), calls=%async_computation.2 | async-start | bytes 22970368 | tf_op jit(solution)/shard_map/psum | solution.py:39
  8.1 7.5 %copy-start.2 = (bf16[256,1024]{1,0:T(8,128)(2,1)S(1)}, bf16[256,1024]{1,0:T(8,128)(2,1)}, u32[]{:S(2)}) copy-start(bf16[256,1024]{1,0:T(8,128)(2,1)} %param.8) | copy-start | bytes 1572868
  8.1 7.5 %copy-start.5 = (bf16[1024,3696]{0,1:T(8,128)(2,1)S(1)}, bf16[1024,3696]{0,1:T(8,128)(2,1)}, u32[]{:S(2)}) copy-start(bf16[1024,3696]{0,1:T(8,128)(2,1)} %param.11) | copy-start | bytes 22708228
  8.1 12.2 %slice-start = ((s8[7569408]{0:T(1024)(128)(4,1)}), s8[4194304]{0:T(1024)(128)(4,1)S(1)}, s32[]{:S(2)}) async-start(s8[7569408]{0:T(1024)(128)(4,1)} %bitcast.28), calls=%async_computation.7 | async-start | bytes 8388608
  15.6 4.1 copy-start.3
  15.6 4.6 %slice-start.1 = ((s8[7569408]{0:T(1024)(128)(4,1)}), s8[3375104]{0:T(1024)(128)(4,1)S(1)}, s32[]{:S(2)}) async-start(s8[7569408]{0:T(1024)(128)(4,1)} %bitcast.28), calls=%async_computation.8 | async-start | bytes 6750208
  20.3 4.2 copy-start.4
  26.0 226.4 %all-reduce.5.cloned.1.call-start = ((), (), s32[]{:S(2)}) async-start(), calls=%async_computation.4 | async-start | bytes 262144 | tf_op jit(solution)/shard_map/psum | solution.py:98
  166.6 2.5 copy-start.1
  169.9 155.5 %reduce-scatter.7.cloned.1.call-start = ((), (), s32[]{:S(2)}) async-start(), calls=%async_computation.6 | async-start | bytes 147456
  171.5 190.8 %all-gather.2.cloned.1.call-start = ((), (), s32[]{:S(2)}) async-start(), calls=%async_computation.5 | async-start | bytes 3145728 | tf_op jit(solution)/shard_map/all_gather | solution.py:10
  173.1 266.4 %reduce-scatter.5.cloned.1.call-start = ((), (), s32[]{:S(2)}) async-start(), calls=%async_computation.3 | async-start | bytes 1179648 | tf_op jit(solution)/shard_map/reduce_scatter | solution.py:77
Sparse Core Ops, SparseCore 0:
  26.1 135.6 all-reduce.2
  170.1 82.2 all-reduce.4
  256.3 69.0 reduce-scatter.6
  327.6 34.6 all-gather.1
  366.3 73.1 reduce-scatter.4
